TPU v7x, 256 devices: a whole 4x4x8 slice. The times are simulated.
256 devices in a mesh: req: 2 (over core), blk: 128 (over z, x, y).
Axes of the slice: x: 4, y: 4, z: 8, core: 2. Of those that a mesh axis runs over, the one named last changes fastest.
Arguments:
- query: bfloat16 [2, 8192, 2048], P('req', 'blk'), may hold values from -64 to 64
- rotated_key_value: bfloat16 [2, 2, 8192, 512], P('req', None, 'blk'), may hold values from -64 to 64
- lengths: int32 [2], P('req'), may hold values from 6144 to 8192, as said below
- block_map: int32 [256], replicated, may hold values from 0 to 255, as said below
- segment_head: int32 [4], replicated, may hold values from 0 to 3, each once
Outputs:
- attended: bfloat16 [2, 8192, 2048], P('req', 'blk')
- cache: bfloat16 [2, 2, 128, 256, 128], P('req', None, 'blk')
Inputs may be any that keep to these rules, and one draw needn't show every extreme that they name: `lengths`: one of the two prompts has exactly 8192 tokens. `block_map`: each prompt block appears once; storage blocks 2d and 2d+1 hold blocks b and 255 - b for some b < 128.
All inputs are finite; a program needn't handle non-finite values.
Results may differ from a plain program's by a relative error of at most 0.007.
Values may be sent and summed in bfloat16 or wider, within the bound.
No kernel may reach another device: no remote copies, remote signals or barrier semaphores. Data moves between devices by JAX's collectives and lax.ppermute only.
A program may use at most 128 MiB of HBM per device.

v0:
```python
import jax
import jax.numpy as jnp
from jax import lax
from jax.sharding import PartitionSpec as P

QUERY_HEADS = 16
KEY_VALUE_HEADS = 4
HEAD_DIMENSION = 128
WINDOW = 4096


def body(query, rotated_key_value, lengths, block_map, segment_head):
    token_index = query.shape[1]
    half_width = token_index // 2
    query_groups = QUERY_HEADS // KEY_VALUE_HEADS
    token_count = lax.axis_size("blk")
    place = lax.axis_index("blk")
    segment_list = token_count // KEY_VALUE_HEADS
    group_repeats = half_width // segment_list
    prompt_blocks = 2 * token_count
    length = lengths[0]
    scale = HEAD_DIMENSION ** (-0.5)
    my_blocks = lax.dynamic_slice_in_dim(block_map, 2 * place, 2)
    qpos = (
        my_blocks[:, None] * half_width + jnp.arange(half_width, dtype=jnp.int32)[None, :]
    ).reshape(token_index)
    query_rows = query[0].reshape(token_index, KEY_VALUE_HEADS, query_groups, HEAD_DIMENSION)
    slot_seg = place % segment_list
    segment_piece = lax.all_gather(rotated_key_value, "blk", axis=2, tiled=True)
    upper_limit = jnp.full((KEY_VALUE_HEADS, query_groups, token_index), -1e30, jnp.float32)
    held = jnp.zeros((2, prompt_blocks, group_repeats, HEAD_DIMENSION), jnp.bfloat16)
    row_indices = segment_piece.shape[2]
    nblock = row_indices // half_width
    owned = jnp.take(block_map, jnp.arange(nblock, dtype=jnp.int32))
    kpos = (owned[:, None] * half_width + jnp.arange(half_width, dtype=jnp.int32)[None, :]).reshape(
        row_indices
    )
    key_rows = segment_piece[0, 0].reshape(row_indices, KEY_VALUE_HEADS, HEAD_DIMENSION)
    value_rows = segment_piece[0, 1].reshape(row_indices, KEY_VALUE_HEADS, HEAD_DIMENSION)
    scores = (
        jnp.einsum("qhgd,khd->hgqk", query_rows, key_rows, preferred_element_type=jnp.float32)
        * scale
    )
    allowed = (kpos[None, :] <= qpos[:, None]) & (kpos[None, :] > qpos[:, None] - WINDOW)
    allowed = allowed & ((kpos[None, :] < length) | (kpos[None, :] == qpos[:, None]))
    allowed = allowed[None, None]
    fresh = jnp.maximum(upper_limit, jnp.max(jnp.where(allowed, scores, -1e30), axis=-1))
    prob = jnp.where(allowed, jnp.exp(scores - fresh[..., None]), 0.0)
    total = jnp.sum(prob, axis=-1)
    summed = jnp.einsum(
        "hgqk,khd->hgqd", prob.astype(jnp.bfloat16), value_rows, preferred_element_type=jnp.float32
    )
    final = (fresh, total, summed, held)
    upper_limit, total, summed, held = final
    result = summed / total[..., None]
    result = jnp.where((qpos < length)[None, None, :, None], result, 0.0)
    attended = (
        result.transpose(2, 0, 1, 3)
        .reshape(1, token_index, QUERY_HEADS * HEAD_DIMENSION)
        .astype(jnp.bfloat16)
    )
    launch_lattice = rotated_key_value[0].reshape(
        2, 2, group_repeats, segment_list, KEY_VALUE_HEADS, HEAD_DIMENSION
    )
    launch_lattice = jnp.take(launch_lattice, segment_head, axis=4)
    outgoing = launch_lattice.transpose(0, 4, 3, 1, 2, 5).reshape(
        2, token_count, 2, group_repeats, HEAD_DIMENSION
    )
    arrived = lax.all_to_all(outgoing, "blk", split_axis=1, concat_axis=1, tiled=True)
    arrived = arrived.reshape(2, prompt_blocks, group_repeats, HEAD_DIMENSION)
    held = (
        jnp.zeros((2, prompt_blocks, group_repeats, HEAD_DIMENSION), jnp.bfloat16)
        .at[:, block_map]
        .set(arrived)
    )
    position = (
        jnp.arange(prompt_blocks, dtype=jnp.int32)[:, None] * group_repeats
        + jnp.arange(group_repeats, dtype=jnp.int32)[None, :]
    ) * segment_list + slot_seg
    held = jnp.where((position < length)[None, :, :, None], held, jnp.zeros((), jnp.bfloat16))
    cache = held.reshape(2, prompt_blocks * group_repeats, HEAD_DIMENSION)[None, :, None]
    return (attended, cache)


def solution(mesh):
    return jax.shard_map(
        body,
        mesh=mesh,
        in_specs=(P("req", "blk", None), P("req", None, "blk", None), P("req"), P(), P()),
        out_specs=(P("req", "blk", None), P("req", None, "blk", None, None)),
        check_vma=False,
    )
```

profile of v0, /device:TPU:1, one launch (start us, length us, event | category | flops | bytes accessed | tf_op | source)
XLA Modules:
  0.0 320.5 jit_solution(6120186794051382634)
XLA Ops:
  7.2 0.0 all-gather.2.cloned.1.call-start
  7.2 1.7 copy.26
  8.9 0.0 all-gather.2.cloned.1.call-update
  8.9 0.9 reshape.238
  9.9 0.7 compare_select_fusion.1
  10.6 0.6 gather_fusion.1
  11.1 0.7 compare_and_fusion
  11.8 0.1 fusion.22
  11.9 0.8 copy.35
  12.7 16.5 %all-to-all-start = ((bf16[2,128,2,1,128]{4,2,0,3,1:T(2,128)(2,1)}), bf16[2,128,2,1,128]{4,2,0,3,1:T(2,128)(2,1)S(1)}, u32[]{:S(2)}, u32[]{:S(2)}) async-start(bf16[2,128,2,1,128]{4,2,0,3,1:T(2,128)(2,1)} %copy.35), calls=%async_computation | async-start | bytes 262144 | tf_op jit(solution)/shard_map/all_to_all | solution.py:69
  29.3 2.0 gather_fusion
  31.3 0.1 iota_add_fusion
  31.4 0.1 add.100
  31.5 0.8 dynamic-slice_multiply_fusion
  32.2 0.1 iota_add_fusion.1
  32.3 0.1 add.96
  33.1 0.8 or_and_fusion
  33.9 1.1 reshape_squeeze.13
  35.0 0.7 compare_select_fusion
  35.7 4.6 %all-to-all-done = bf16[2,128,2,1,128]{4,2,0,3,1:T(2,128)(2,1)S(1)} async-done(((bf16[2,128,2,1,128]{4,2,0,3,1:T(2,128)(2,1)}), bf16[2,128,2,1,128]{4,2,0,3,1:T(2,128)(2,1)S(1)}, u32[]{:S(2)}, u32[]{:S(2)}) %all-to-all-start) | async-done | bytes 131104 | tf_op jit(solution)/shard_map/all_to_all | solution.py:69
  40.3 0.1 copy.36
  40.4 0.1 copy.37
  40.5 0.1 broadcast.181
  40.6 7.2 %scatter_fusion = bf16[2,256,128]{2,0,1:T(2,128)(2,1)S(1)} fusion(bf16[2,256,128]{2,0,1:T(2,128)(2,1)S(1)} %broadcast.181, s32[256]{0:T(256)S(1)} %compare_select_fusion, bf16[256,2,128]{2,1,0:T(2,128)(2,1)S(1)} %copy.37), kind=kCustom, calls=%fused_computation.2 | custom fusion | bytes 394240 | tf_op jit(solution)/shard_map/scatter | solution.py:74
  47.8 0.3 fusion.23
  48.1 0.7 copy.38
  48.8 117.2 %all-gather.2.cloned.1.call-done = bf16[1,2,8192,512]{3,1,0,2:T(2,128)(2,1)} async-done(((bf16[1,2,64,512]{3,1,0,2:T(2,128)(2,1)}), bf16[1,2,8192,512]{3,1,0,2:T(2,128)(2,1)}) %all-gather.2.cloned.1.call-update) | async-done | bytes 16777232 | tf_op jit(solution)/shard_map/all_gather | solution.py:29
  166.0 32.7 %fusion.27 = (bf16[1,1,8192,512]{3,1,0,2:T(2,128)(2,1)}, bf16[1,1,8192,512]{3,1,0,2:T(2,128)(2,1)}) fusion(bf16[1,2,8192,512]{3,1,0,2:T(2,128)(2,1)} %all-gather.2.cloned.1.call-done), kind=kLoop, calls=%fused_computation.40 | loop fusion | bytes 33554432 | tf_op jit(solution)/shard_map/slice | solution.py:38
  198.7 33.4 %copy.46 = bf16[1,1,8192,512]{2,3,1,0:T(8,128)(2,1)} copy(bf16[1,1,8192,512]{3,1,0,2:T(2,128)(2,1)} %get-tuple-element.11) | data formatting | bytes 16777216
  232.1 33.3 %copy.45 = bf16[1,1,8192,512]{2,3,1,0:T(8,128)(2,1)} copy(bf16[1,1,8192,512]{3,1,0,2:T(2,128)(2,1)} %get-tuple-element.10) | data formatting | bytes 16777216
  265.4 16.0 %fusion = (f32[4,4,64]{2,1,0:T(4,128)S(1)}, f32[4,8192,64,4]{1,2,3,0:T(8,128)}) fusion(pred[64,8192]{1,0:T(8,128)(4,1)S(1)} %or_and_fusion, bf16[8192,4,128,1]{0,2,3,1:T(8,128)(2,1)} %bitcast.67, bf16[64,4,4,128]{3,2,1,0:T(4,128)(2,1)S(1)} %reshape_squeeze.13), kind=kOutput, calls=%fused_computation.5 | convolution fusion | flops 2172648448 | bytes 42733568 | tf_op jit(solution)/shard_map/qhgd,khd->hgqk/dot_general | solution.py:41
  281.4 15.2 %fusion.3 = f32[4,4,64]{2,1,0:T(4,128)S(1)} fusion(f32[4,8192,64,4]{1,2,3,0:T(8,128)} %get-tuple-element.13, f32[4,4,64]{2,1,0:T(4,128)S(1)} %broadcast_maximum_fusion, pred[64,8192]{1,0:T(8,128)(4,1)S(1)} %or_and_fusion), kind=kLoop, calls=%fused_computation.8 | loop fusion | flops 33553408 | bytes 34086912 | tf_op jit(solution)/shard_map/reduce_sum | solution.py:49
  296.6 15.9 %fusion.17 = bf16[64,4,4,128]{3,0,2,1:T(8,128)(2,1)S(1)} fusion(bf16[8192,4,128,1]{0,2,3,1:T(8,128)(2,1)} %bitcast.68, f32[4,8192,64,4]{1,2,3,0:T(8,128)} %get-tuple-element.13, f32[4,4,64]{2,1,0:T(4,128)S(1)} %broadcast_maximum_fusion, pred[64,8192]{1,0:T(8,128)(4,1)S(1)} %or_and_fusion, f32[64,4,4]{0,2,1:T(4,128)S(1)} %bitcast.71, ...), kind=kOutput, calls=%fused_computation.16 | convolution fusion | flops 2181431296 | bytes 42737728 | tf_op jit(solution)/shard_map/hgqk,khd->hgqd/dot_general | solution.py:50
  312.6 0.2 copy.32
  312.8 0.9 convert_element_type.19
  (11 shorter events, 0.1 us)
Async XLA Ops:
  7.2 158.8 %all-gather.2.cloned.1.call-start = ((), (), s32[]{:S(2)}) async-start(), calls=%async_computation.1 | async-start | bytes 16908288 | tf_op jit(solution)/shard_map/all_gather | solution.py:29
  12.7 27.6 %all-to-all-start = ((bf16[2,128,2,1,128]{4,2,0,3,1:T(2,128)(2,1)}), bf16[2,128,2,1,128]{4,2,0,3,1:T(2,128)(2,1)S(1)}, u32[]{:S(2)}, u32[]{:S(2)}) async-start(bf16[2,128,2,1,128]{4,2,0,3,1:T(2,128)(2,1)} %copy.35), calls=%async_computation | async-start | bytes 262144 | tf_op jit(solution)/shard_map/all_to_all | solution.py:69
Sparse Core Ops, SparseCore 0:
  12.0 153.9 all-gather.1
where the time goes:
time: 323 us; the launch traced here: 321 us
  waiting for transfers between devices  122 us (38%)
  local copies, waits for them, and re-layouts  116 us (36%)
  matrix products  31.9 us (10%)
  other arithmetic  19.4 us (6%)
  starting transfers between devices  16.6 us (5%)
  between operations  14.9 us (5%)
    all_gather x1, waiting for transfers between devices, body(): segment_piece = lax.all_gather(rotated_key_value, 'blk', axis=2, tiled=True)  117 us
    unnamed x4, local copies, waits for them, and re-layouts  69.1 us
    slice x1, local copies, waits for them, and re-layouts, body(): segment_piece[0, 0].reshape(row_indices, KEY_VALUE_HEADS, HEAD_DIMENSION)  32.7 us
    all_to_all x1, starting transfers between devices, body(): lax.all_to_all(outgoing, 'blk', split_axis=1, concat_axis=1, tiled=True)  16.5 us
    dot_general x1, matrix products, body(): jnp.einsum('qhgd,khd->hgqk', query_rows, key_rows, preferred_element_type...  16 us
    dot_general x1, matrix products, body(): jnp.einsum('hgqk,khd->hgqd', prob.astype(jnp.bfloat16), value_rows, prefe...  15.9 us
    reduce_sum x1, other arithmetic, body(): total = jnp.sum(prob, axis=-1)  15.2 us
    scatter x1, local copies, waits for them, and re-layouts, body(): held = jnp.zeros((2, prompt_blocks, group_repeats, HEAD_DIMENSION), jnp.b...  7.17 us
  transfers between devices with their start and end apart: 2, of which 2 were waited for; matrix products, arithmetic and copies ran while one was open for 6% of the time, Pallas kernels for 0%

commit v1 on v0

--- a/solution.py
+++ b/solution.py
@@ -26,7 +26,9 @@
     ).reshape(token_index)
     query_rows = query[0].reshape(token_index, KEY_VALUE_HEADS, query_groups, HEAD_DIMENSION)
     slot_seg = place % segment_list
-    segment_piece = lax.all_gather(rotated_key_value, "blk", axis=2, tiled=True)
+    segment_piece = jnp.concatenate(
+        lax.all_to_all(jnp.stack([rotated_key_value] * lax.axis_size("blk")), "blk", 0, 0), axis=2
+    )
     upper_limit = jnp.full((KEY_VALUE_HEADS, query_groups, token_index), -1e30, jnp.float32)
     held = jnp.zeros((2, prompt_blocks, group_repeats, HEAD_DIMENSION), jnp.bfloat16)
     row_indices = segment_piece.shape[2]

time: 323 us -> 503 us (1.56)
  waiting for transfers between devices: 122 us -> 354 us
  local copies, waits for them, and re-layouts: 116 us -> 56.8 us
  blocking collectives: 0 us -> 27.4 us
  between operations: 14.9 us -> 1.54 us
  starting transfers between devices: 16.6 us -> 7.89 us
    all_to_all x1, waiting for transfers between devices: 4.62 us -> 354 us  [body(): lax.all_to_all(jnp.stack([rotated_key_value] * lax.axis_size('blk')), 'bl...]
    all_gather x1 -> x0, waiting for transfers between devices: 117 us -> none  [body(): segment_piece = lax.all_gather(rotated_key_value, 'blk', axis=2, tiled=True)]
    unnamed x4 -> x5, local copies, waits for them, and re-layouts: 69.1 us -> 0.68 us
    all_to_all x0 -> x1, blocking collectives: none -> 27.4 us  [body(): lax.all_to_all(outgoing, 'blk', split_axis=1, concat_axis=1, tiled=True)]
    slice x1 -> x2, local copies, waits for them, and re-layouts: 32.7 us -> 17.3 us  [body(): segment_piece[0, 0].reshape(row_indices, KEY_VALUE_HEADS, HEAD_DIMENSION)]
    slice x0 -> x1, local copies, waits for them, and re-layouts: none -> 11.3 us  [body(): segment_piece[0, 1].reshape(row_indices, KEY_VALUE_HEADS, HEAD_DIMENSION)]
    all_to_all x1, starting transfers between devices: 16.5 us -> 7.89 us  [body(): lax.all_to_all(jnp.stack([rotated_key_value] * lax.axis_size('blk')), 'bl...]
    all_to_all x0 -> x1, local copies, waits for them, and re-layouts: none -> 8.2 us  [body(): lax.all_to_all(jnp.stack([rotated_key_value] * lax.axis_size('blk')), 'bl...]
  transfers between devices with their start and end apart: 2 -> 1, of which waited for: 2 -> 1; matrix products, arithmetic and copies ran while one was open for 6% -> 2% of each run, Pallas kernels for 0% -> 0%
where the time goes in v1:
time: 503 us; the launch traced here: 498 us
  waiting for transfers between devices  354 us (70%)
  local copies, waits for them, and re-layouts  56.8 us (11%)
  matrix products  31.9 us (6%)
  blocking collectives  27.4 us (5%)
  other arithmetic  18 us (4%)
  starting transfers between devices  7.89 us (2%)
    all_to_all x1, waiting for transfers between devices, body(): lax.all_to_all(jnp.stack([rotated_key_value] * lax.axis_size('blk')), 'bl...  354 us
    all_to_all x1, blocking collectives, body(): lax.all_to_all(outgoing, 'blk', split_axis=1, concat_axis=1, tiled=True)  27.4 us
    slice x2, local copies, waits for them, and re-layouts, body(): segment_piece[0, 0].reshape(row_indices, KEY_VALUE_HEADS, HEAD_DIMENSION)  17.3 us
    dot_general x1, matrix products, body(): jnp.einsum('qhgd,khd->hgqk', query_rows, key_rows, preferred_element_type...  16 us
    dot_general x1, matrix products, body(): jnp.einsum('hgqk,khd->hgqd', prob.astype(jnp.bfloat16), value_rows, prefe...  15.9 us
    reduce_sum x1, other arithmetic, body(): total = jnp.sum(prob, axis=-1)  15.2 us
    slice x1, local copies, waits for them, and re-layouts, body(): segment_piece[0, 1].reshape(row_indices, KEY_VALUE_HEADS, HEAD_DIMENSION)  11.3 us
  transfers between devices with their start and end apart: 1, of which 1 were waited for; matrix products, arithmetic and copies ran while one was open for 2% of the time, Pallas kernels for 0%

profile of v1, /device:TPU:1, one launch (start us, length us, event | category | flops | bytes accessed | tf_op | source)
XLA Modules:
  0.0 497.6 jit_solution(10395480810617388527)
XLA Ops:
  0.6 0.7 compare_select_fusion.1
  1.3 0.7 compare_and_fusion
  2.0 0.9 reshape.249
  2.9 0.6 gather_fusion.1
  3.5 0.1 fusion.22
  3.6 0.1 copy.37
  3.8 27.4 %all_to_all.10 = bf16[2,128,2,1,128]{4,2,0,3,1:T(2,128)(2,1)S(1)} all-to-all(bf16[2,128,2,1,128]{4,2,0,3,1:T(2,128)(2,1)S(1)} %copy.37), channel_id=1, replica_groups=mesh['req'=2,'blk'=128] {'blk'}, dimensions={1} | all-to-all | bytes 262144 | tf_op jit(solution)/shard_map/all_to_all | solution.py:71
  31.1 6.7 %stack.2 = bf16[128,1,2,64,512]{4,3,2,1,0:T(8,128)(2,1)} broadcast(bf16[2,64,512]{2,1,0:T(8,128)(2,1)} %bitcast.74), dimensions={2,3,4} | broadcast | bytes 16908288 | tf_op jit(solution)/shard_map/stack | solution.py:30
  37.8 0.0 copy-start
  37.8 0.0 copy-start.1
  37.9 7.9 %all-to-all-start = ((bf16[128,1,2,64,512]{4,3,2,1,0:T(8,128)(2,1)}), bf16[128,1,2,64,512]{4,3,2,1,0:T(8,128)(2,1)}, u32[]{:S(2)}, u32[]{:S(2)}) async-start(bf16[128,1,2,64,512]{4,3,2,1,0:T(8,128)(2,1)} %stack.2), calls=%async_computation | async-start | bytes 33554432 | tf_op jit(solution)/shard_map/all_to_all | solution.py:30
  45.8 0.0 copy-done
  45.8 1.9 gather_fusion
  47.8 0.1 iota_add_fusion
  47.9 0.1 add.100
  48.0 0.1 dynamic-slice_multiply_fusion
  48.0 0.1 iota_add_fusion.1
  48.1 0.1 add.96
  48.8 0.0 copy-done.1
  48.9 0.2 reshape_squeeze.13
  49.1 0.8 or_and_fusion
  49.9 0.1 copy.38
  50.0 0.1 copy.39
  50.1 0.1 broadcast.184
  50.2 7.2 %scatter_fusion = bf16[2,256,128]{2,0,1:T(2,128)(2,1)S(1)} fusion(bf16[2,256,128]{2,0,1:T(2,128)(2,1)S(1)} %broadcast.184, s32[256]{0:T(256)S(1)} %compare_select_fusion, bf16[256,2,128]{2,1,0:T(2,128)(2,1)S(1)} %copy.39), kind=kCustom, calls=%fused_computation.2 | custom fusion | bytes 394240 | tf_op jit(solution)/shard_map/scatter | solution.py:76
  57.4 0.3 fusion.23
  57.7 0.7 copy.40
  58.4 354.1 %all-to-all-done = bf16[128,1,2,64,512]{4,3,2,1,0:T(8,128)(2,1)} async-done(((bf16[128,1,2,64,512]{4,3,2,1,0:T(8,128)(2,1)}), bf16[128,1,2,64,512]{4,3,2,1,0:T(8,128)(2,1)}, u32[]{:S(2)}, u32[]{:S(2)}) %all-to-all-start) | async-done | bytes 16777248 | tf_op jit(solution)/shard_map/all_to_all | solution.py:30
  412.5 8.2 %copy.28 = bf16[128,1,2,64,512]{4,3,0,2,1:T(8,128)(2,1)S(1)} copy(bf16[128,1,2,64,512]{4,3,2,1,0:T(8,128)(2,1)} %all-to-all-done) | data formatting | bytes 33554432 | tf_op jit(solution)/shard_map/all_to_all | solution.py:30
  420.7 6.0 %fusion.27 = (bf16[1,1,8192,512]{3,2,1,0:T(8,128)(2,1)}, bf16[1,1,8192,512]{3,2,1,0:T(8,128)(2,1)}) fusion(bf16[1,2,8192,512]{3,2,1,0:T(8,128)(2,1)S(1)} %bitcast.71), kind=kLoop, calls=%fused_computation.40 | loop fusion | bytes 33554432 | tf_op jit(solution)/shard_map/slice | solution.py:40
  426.7 11.3 %copy.32 = bf16[1,1,8192,512]{2,3,1,0:T(8,128)(2,1)} copy(bf16[1,1,8192,512]{3,2,1,0:T(8,128)(2,1)} %get-tuple-element.11) | data formatting | bytes 16777216 | tf_op jit(solution)/shard_map/slice | solution.py:41
  438.0 11.3 %copy.29 = bf16[1,1,8192,512]{2,3,1,0:T(8,128)(2,1)} copy(bf16[1,1,8192,512]{3,2,1,0:T(8,128)(2,1)} %get-tuple-element.10) | data formatting | bytes 16777216 | tf_op jit(solution)/shard_map/slice | solution.py:40
  449.3 16.0 %fusion = (f32[4,4,64]{2,1,0:T(4,128)S(1)}, f32[4,8192,64,4]{1,2,3,0:T(8,128)}) fusion(pred[64,8192]{1,0:T(8,128)(4,1)S(1)} %or_and_fusion, bf16[8192,4,128,1]{0,2,3,1:T(8,128)(2,1)} %bitcast.72, bf16[64,4,4,128]{3,2,1,0:T(4,128)(2,1)S(1)} %reshape_squeeze.13), kind=kOutput, calls=%fused_computation.5 | convolution fusion | flops 2172648448 | bytes 42733568 | tf_op jit(solution)/shard_map/qhgd,khd->hgqk/dot_general | solution.py:43
  465.3 15.2 %fusion.3 = f32[4,4,64]{2,1,0:T(4,128)S(1)} fusion(f32[4,8192,64,4]{1,2,3,0:T(8,128)} %get-tuple-element.13, f32[4,4,64]{2,1,0:T(4,128)S(1)} %broadcast_maximum_fusion, pred[64,8192]{1,0:T(8,128)(4,1)S(1)} %or_and_fusion), kind=kLoop, calls=%fused_computation.8 | loop fusion | flops 33553408 | bytes 34086912 | tf_op jit(solution)/shard_map/reduce_sum | solution.py:51
  480.5 15.9 %fusion.17 = bf16[64,4,4,128]{3,0,2,1:T(8,128)(2,1)S(1)} fusion(bf16[8192,4,128,1]{0,2,3,1:T(8,128)(2,1)} %bitcast.73, f32[4,8192,64,4]{1,2,3,0:T(8,128)} %get-tuple-element.13, f32[4,4,64]{2,1,0:T(4,128)S(1)} %broadcast_maximum_fusion, pred[64,8192]{1,0:T(8,128)(4,1)S(1)} %or_and_fusion, f32[64,4,4]{0,2,1:T(4,128)S(1)} %bitcast.77, ...), kind=kOutput, calls=%fused_computation.16 | convolution fusion | flops 2181431296 | bytes 42737728 | tf_op jit(solution)/shard_map/hgqk,khd->hgqd/dot_general | solution.py:52
  496.5 0.2 copy.34
  496.7 0.9 convert_element_type.19
  (12 shorter events, 0.1 us)
Async XLA Ops:
  37.8 7.9 %copy-start = (s32[256]{0:T(256)S(1)}, s32[256]{0:T(256)}, u32[]{:S(2)}) copy-start(s32[256]{0:T(256)} %param.8) | copy-start | bytes 3076
  37.8 11.0 %copy-start.1 = (bf16[1,64,2048]{2,1,0:T(8,128)(2,1)S(1)}, bf16[1,64,2048]{2,1,0:T(8,128)(2,1)}, u32[]{:S(2)}) copy-start(bf16[1,64,2048]{2,1,0:T(8,128)(2,1)} %param.5) | copy-start | bytes 786436
  37.9 374.6 %all-to-all-start = ((bf16[128,1,2,64,512]{4,3,2,1,0:T(8,128)(2,1)}), bf16[128,1,2,64,512]{4,3,2,1,0:T(8,128)(2,1)}, u32[]{:S(2)}, u32[]{:S(2)}) async-start(bf16[128,1,2,64,512]{4,3,2,1,0:T(8,128)(2,1)} %stack.2), calls=%async_computation | async-start | bytes 33554432 | tf_op jit(solution)/shard_map/all_to_all | solution.py:30
